TPU v7x, 256 devices: a whole 4x4x8 slice. The times are simulated.
256 devices in a mesh: row: 16 (over x, z_hi, core), col: 16 (over z_lo, y).
Axes of the slice: x: 4, y: 4, z: 8 (z_hi: 2, z_lo: 4; z = z_hi * 4 + z_lo), core: 2. Of those that a mesh axis runs over, the one named last changes fastest.
Arguments:
- ancestor_inverse: bfloat16 [24576, 24576], P('row', 'col'), may hold values from -0.0390625 to 0.0390625
- panels: bfloat16 [24576, 3, 512], P(('row', 'col')), may hold values from -1.1953125 to 1.1953125
- diag_inverse: float32 [3, 512, 512], replicated, may hold values from -6 to 6
- tile_mask: int32 [3, 192], replicated, may hold values 0 or 1
Outputs:
- off_diagonal: float32 [24576, 3, 512], P(('row', 'col'))
- diagonal: float32 [3, 512, 512], replicated
All inputs are finite; a program needn't handle non-finite values.
Results may differ from a plain program's by a relative error of at most 0.0003.
Values may be sent and summed in bfloat16 or wider, within the bound.
No kernel may reach another device: no remote copies, remote signals or barrier semaphores. Data moves between devices by JAX's collectives and lax.ppermute only.
A program may use at most 192 MiB of HBM per device.

v0:
```python
import jax
import jax.numpy as jnp
from jax import lax
from jax.sharding import PartitionSpec as P

TILE = 128
ALL = ("row", "col")


def body(ancestor_inverse, panels, diag_inverse, tile_mask):
    rows, cols = (lax.axis_size("row"), lax.axis_size("col"))
    row_index, col_index = (lax.axis_index("row"), lax.axis_index("col"))
    kept, count, width = panels.shape
    start = (row_index * cols + col_index) * kept
    tile_of = (start + jnp.arange(kept)) // TILE
    own_mask = jnp.take(tile_mask, tile_of, axis=1).astype(jnp.bfloat16)
    masked = jnp.swapaxes(panels, 0, 1) * own_mask[:, :, None]
    flip = [(i * cols + j, j * cols + i) for i in range(rows) for j in range(cols)]
    turned = lax.ppermute(masked, ALL, flip)
    blocks = []
    for p in range(count):
        gathered = lax.all_gather(turned[p], "row", axis=0, tiled=True)
        partial = jnp.dot(ancestor_inverse, gathered, preferred_element_type=jnp.float32)
        summed = lax.psum_scatter(partial, "col", scatter_dimension=0, tiled=True)
        blocks.append(-summed)
    off_diagonal = jnp.stack(blocks)
    schur = jnp.einsum(
        "pma,pmb->pab", masked.astype(jnp.float32), off_diagonal, precision=lax.Precision.HIGHEST
    )
    lines = schur.reshape(count * width, width)
    share = lax.psum_scatter(lines, "col", scatter_dimension=0, tiled=True)
    share = lax.psum(share, "row")
    total = lax.all_gather(share, "col", axis=0, tiled=True)
    return (jnp.swapaxes(off_diagonal, 0, 1), diag_inverse - total.reshape(schur.shape))


def solution(mesh):
    placed = (P("row", "col"), P(ALL, None, None), P(), P())
    return jax.shard_map(
        body, mesh=mesh, in_specs=placed, out_specs=(P(ALL, None, None), P()), check_vma=False
    )
```

profile of v0, /device:TPU:2, one launch (start us, length us, event | category | flops | bytes accessed | tf_op | source)
XLA Modules:
  0.0 855.5 jit_solution(13379166648206793179)
XLA Ops:
  8.9 1.1 bitcast_multiply_fusion
  10.0 3.8 collective-permute-start
  13.8 32.1 %collective-permute-done = bf16[3,96,512]{2,1,0:T(8,128)(2,1)S(1)} collective-permute-done((bf16[3,96,512]{2,1,0:T(8,128)(2,1)S(1)}, bf16[3,96,512]{2,1,0:T(8,128)(2,1)S(1)}, u32[]{:S(2)}, u32[]{:S(2)}) %collective-permute-start) | collective-permute-done | bytes 294944 | tf_op jit(solution)/shard_map/ppermute | solution.py:19
  48.1 61.7 %all-gather.14.cloned.1.call-done = bf16[1,1536,512]{2,1,0:T(8,128)(2,1)} async-done(((bf16[1,96,512]{2,1,0:T(8,128)(2,1)}), bf16[1,1536,512]{2,1,0:T(8,128)(2,1)}) %all-gather.14.cloned.1.call-update) | async-done | bytes 1572880 | tf_op jit(solution)/shard_map/all_gather | solution.py:22
  109.8 5.0 convolution_bitcast_fusion
  114.8 2.4 copy.19
  117.3 50.4 %all-gather.12.cloned.1.call-done = bf16[1,1536,512]{2,1,0:T(8,128)(2,1)} async-done(((bf16[1,96,512]{2,1,0:T(8,128)(2,1)}), bf16[1,1536,512]{2,1,0:T(8,128)(2,1)}) %all-gather.12.cloned.1.call-update) | async-done | bytes 1572880 | tf_op jit(solution)/shard_map/all_gather | solution.py:22
  167.7 5.0 convolution_bitcast_fusion.1
  172.7 2.4 copy.17
  175.1 51.0 %all-gather.10.cloned.1.call-done = bf16[1,1536,512]{2,1,0:T(8,128)(2,1)} async-done(((bf16[1,96,512]{2,1,0:T(8,128)(2,1)}), bf16[1,1536,512]{2,1,0:T(8,128)(2,1)}) %all-gather.10.cloned.1.call-update) | async-done | bytes 1572880 | tf_op jit(solution)/shard_map/all_gather | solution.py:22
  226.1 5.0 convolution_bitcast_fusion.2
  231.2 2.4 copy.15
  233.6 83.0 %reduce-scatter.17.cloned.1.call-done = f32[96,512]{1,0:T(8,128)} async-done(((f32[1536,512]{1,0:T(8,128)}), f32[96,512]{1,0:T(8,128)}) %reduce-scatter.17.cloned.1.call-update) | async-done | bytes 196624 | tf_op jit(solution)/shard_map/reduce_scatter | solution.py:24
  316.6 0.9 negate_bitcast_fusion
  317.5 89.1 %reduce-scatter.15.cloned.1.call-done = f32[96,512]{1,0:T(8,128)} async-done(((f32[1536,512]{1,0:T(8,128)}), f32[96,512]{1,0:T(8,128)}) %reduce-scatter.15.cloned.1.call-update) | async-done | bytes 196624 | tf_op jit(solution)/shard_map/reduce_scatter | solution.py:24
  406.6 0.9 negate_bitcast_fusion.1
  407.6 89.0 %reduce-scatter.13.cloned.1.call-done = f32[96,512]{1,0:T(8,128)} async-done(((f32[1536,512]{1,0:T(8,128)}), f32[96,512]{1,0:T(8,128)}) %reduce-scatter.13.cloned.1.call-update) | async-done | bytes 196624 | tf_op jit(solution)/shard_map/reduce_scatter | solution.py:24
  496.6 0.9 negate_bitcast_fusion.2
  498.2 3.1 fusion.3
  501.4 87.6 %reduce-scatter.11.cloned.1.call-done = f32[96,512]{1,0:T(8,128)} async-done(((f32[1536,512]{1,0:T(8,128)}), f32[96,512]{1,0:T(8,128)}) %reduce-scatter.11.cloned.1.call-update) | async-done | bytes 196624 | tf_op jit(solution)/shard_map/reduce_scatter | solution.py:31
  589.1 163.7 %all-reduce.2.cloned.1.call-done = f32[96,512]{1,0:T(8,128)} async-done(((f32[96,512]{1,0:T(8,128)}), f32[96,512]{1,0:T(8,128)}) %all-reduce.2.cloned.1.call-update) | async-done | bytes 196624 | tf_op jit(solution)/shard_map/psum | solution.py:32
  752.9 1.8 fusion.4
  754.6 90.0 %all-gather.8.cloned.1.call-done = f32[1536,512]{1,0:T(8,128)} async-done(((f32[96,512]{1,0:T(8,128)}), f32[1536,512]{1,0:T(8,128)}) %all-gather.8.cloned.1.call-update) | async-done | bytes 3145744 | tf_op jit(solution)/shard_map/all_gather | solution.py:33
  844.7 4.3 sub.13
  (30 shorter events, 4.9 us)
Async XLA Ops:
  7.2 102.6 %all-gather.14.cloned.1.call-start = ((), (), s32[]{:S(2)}) async-start(), calls=%async_computation.9 | async-start | bytes 1671168 | tf_op jit(solution)/shard_map/all_gather | solution.py:22
  10.0 35.9 %collective-permute-start = (bf16[3,96,512]{2,1,0:T(8,128)(2,1)S(1)}, bf16[3,96,512]{2,1,0:T(8,128)(2,1)S(1)}, u32[]{:S(2)}, u32[]{:S(2)}) collective-permute-start(bf16[3,96,512]{2,1,0:T(8,128)(2,1)S(1)} %bitcast_multiply_fusion), channel_id=1, source_target_pairs={{0,0},{1,16},{2,32},{3,48},{4,64},{5,80},{6,96},{7,112},{8,128},{9... | collective-permute-start | bytes 884744 | tf_op jit(solution)/shard_map/ppermute | solution.py:19
  46.6 121.1 %all-gather.12.cloned.1.call-start = ((), (), s32[]{:S(2)}) async-start(), calls=%async_computation.8 | async-start | bytes 1671168 | tf_op jit(solution)/shard_map/all_gather | solution.py:22
  47.3 178.8 %all-gather.10.cloned.1.call-start = ((), (), s32[]{:S(2)}) async-start(), calls=%async_computation.7 | async-start | bytes 1671168 | tf_op jit(solution)/shard_map/all_gather | solution.py:22
  48.1 268.5 %reduce-scatter.17.cloned.1.call-start = ((), (), s32[]{:S(2)}) async-start(), calls=%async_computation.12 | async-start | bytes 3342336 | tf_op jit(solution)/shard_map/reduce_scatter | solution.py:24
  117.2 289.4 %reduce-scatter.15.cloned.1.call-start = ((), (), s32[]{:S(2)}) async-start(), calls=%async_computation.11 | async-start | bytes 3342336 | tf_op jit(solution)/shard_map/reduce_scatter | solution.py:24
  175.1 321.5 %reduce-scatter.13.cloned.1.call-start = ((), (), s32[]{:S(2)}) async-start(), calls=%async_computation.10 | async-start | bytes 3342336 | tf_op jit(solution)/shard_map/reduce_scatter | solution.py:24
  233.6 355.4 %reduce-scatter.11.cloned.1.call-start = ((), (), s32[]{:S(2)}) async-start(), calls=%async_computation.4 | async-start | bytes 3342336 | tf_op jit(solution)/shard_map/reduce_scatter | solution.py:31
  497.5 0.7 copy-start.1
  501.3 343.4 %copy-start = (f32[3,512,512]{2,1,0:T(8,128)S(1)}, f32[3,512,512]{2,1,0:T(8,128)}, u32[]{:S(2)}) copy-start(f32[3,512,512]{2,1,0:T(8,128)} %param.6) | copy-start | bytes 9437188
  501.3 251.5 %all-reduce.2.cloned.1.call-start = ((), (), s32[]{:S(2)}) async-start(), calls=%async_computation.5 | async-start | bytes 393216 | tf_op jit(solution)/shard_map/psum | solution.py:32
  589.0 255.6 %all-gather.8.cloned.1.call-start = ((), (), s32[]{:S(2)}) async-start(), calls=%async_computation.6 | async-start | bytes 3342336 | tf_op jit(solution)/shard_map/all_gather | solution.py:33
Sparse Core Ops, SparseCore 0:
  46.7 63.0 all-gather.13
  112.5 55.1 all-gather.11
  170.9 55.1 all-gather.9
  229.1 87.4 reduce-scatter.16
  319.0 87.5 reduce-scatter.14
  409.0 87.5 reduce-scatter.12
  501.5 87.5 reduce-scatter.10
  591.6 161.1 all-reduce.1
  754.8 89.8 all-gather.7
where the time goes:
time: 856 us
  waiting for transfers between devices  799 us (93%)
  matrix products  18.1 us (2%)
  between operations  13.9 us (2%)
  other arithmetic  10.1 us (1%)
  local copies, waits for them, and re-layouts  10 us (1%)
    reduce_scatter x3, waiting for transfers between devices, body(): summed = lax.psum_scatter(partial, 'col', scatter_dimension=0, tiled=True)  261 us
    psum x1, waiting for transfers between devices, body(): share = lax.psum(share, 'row')  164 us
    all_gather x3, waiting for transfers between devices, body(): gathered = lax.all_gather(turned[p], 'row', axis=0, tiled=True)  163 us
    all_gather x1, waiting for transfers between devices, body(): total = lax.all_gather(share, 'col', axis=0, tiled=True)  90 us
    reduce_scatter x1, waiting for transfers between devices, body(): share = lax.psum_scatter(lines, 'col', scatter_dimension=0, tiled=True)  87.6 us
    ppermute x1, waiting for transfers between devices, body(): turned = lax.ppermute(masked, ALL, flip)  32.1 us
  transfers between devices with their start and end apart: 10, of which 10 were waited for; matrix products, arithmetic and copies ran while one was open for 3% of the time, Pallas kernels for 0%

commit v1 on v0

--- a/solution.py
+++ b/solution.py
@@ -19,7 +19,9 @@
     turned = lax.ppermute(masked, ALL, flip)
     blocks = []
     for p in range(count):
-        gathered = lax.all_gather(turned[p], "row", axis=0, tiled=True)
+        gathered = jnp.concatenate(
+            lax.all_to_all(jnp.stack([turned[p]] * lax.axis_size("row")), "row", 0, 0), axis=0
+        )
         partial = jnp.dot(ancestor_inverse, gathered, preferred_element_type=jnp.float32)
         summed = lax.psum_scatter(partial, "col", scatter_dimension=0, tiled=True)
         blocks.append(-summed)

time: 856 us -> 755 us (0.88)
  waiting for transfers between devices: 799 us -> 568 us
  blocking collectives: 0 us -> 132 us
    all_gather x3 -> x0, waiting for transfers between devices: 163 us -> none  [body(): gathered = lax.all_gather(turned[p], 'row', axis=0, tiled=True)]
    all_to_all x0 -> x3, blocking collectives: none -> 132 us  [body(): lax.all_to_all(jnp.stack([turned[p]] * lax.axis_size('row')), 'row', 0, 0)]
    reduce_scatter x3, waiting for transfers between devices: 261 us -> 195 us  [body(): summed = lax.psum_scatter(partial, 'col', scatter_dimension=0, tiled=True)]
  transfers between devices with their start and end apart: 10 -> 7, of which waited for: 10 -> 7; matrix products, arithmetic and copies ran while one was open for 3% -> 2% of each run, Pallas kernels for 0% -> 0%
where the time goes in v1:
time: 755 us
  waiting for transfers between devices  568 us (75%)
  blocking collectives  132 us (17%)
  matrix products  15 us (2%)
  between operations  14.2 us (2%)
  local copies, waits for them, and re-layouts  11.2 us (1%)
  other arithmetic  10.3 us (1%)
    reduce_scatter x3, waiting for transfers between devices, body(): summed = lax.psum_scatter(partial, 'col', scatter_dimension=0, tiled=True)  195 us
    psum x1, waiting for transfers between devices, body(): share = lax.psum(share, 'row')  164 us
    all_to_all x3, blocking collectives, body(): lax.all_to_all(jnp.stack([turned[p]] * lax.axis_size('row')), 'row', 0, 0)  132 us
    all_gather x1, waiting for transfers between devices, body(): total = lax.all_gather(share, 'col', axis=0, tiled=True)  89.9 us
    reduce_scatter x1, waiting for transfers between devices, body(): share = lax.psum_scatter(lines, 'col', scatter_dimension=0, tiled=True)  87.6 us
    ppermute x1, waiting for transfers between devices, body(): turned = lax.ppermute(masked, ALL, flip)  32.1 us
  transfers between devices with their start and end apart: 7, of which 7 were waited for; matrix products, arithmetic and copies ran while one was open for 2% of the time, Pallas kernels for 0%

profile of v1, /device:TPU:2, one launch (start us, length us, event | category | flops | bytes accessed | tf_op | source)
XLA Modules:
  0.0 754.8 jit_solution(7364839685606994076)
XLA Ops:
  8.9 1.2 bitcast_multiply_fusion
  10.1 3.9 collective-permute-start
  14.0 32.1 %collective-permute-done = bf16[3,96,512]{2,1,0:T(8,128)(2,1)S(1)} collective-permute-done((bf16[3,96,512]{2,1,0:T(8,128)(2,1)S(1)}, bf16[3,96,512]{2,1,0:T(8,128)(2,1)S(1)}, u32[]{:S(2)}, u32[]{:S(2)}) %collective-permute-start) | collective-permute-done | bytes 294944 | tf_op jit(solution)/shard_map/ppermute | solution.py:19
  46.9 46.6 %all_to_all.15 = bf16[16,96,512]{2,1,0:T(8,128)(2,1)S(1)} all-to-all(bf16[16,96,512]{2,1,0:T(8,128)(2,1)S(1)} %stack.21), channel_id=1, replica_groups=mesh['row'=16,'col'=16] {'row'}, dimensions={0} | all-to-all | bytes 3145728 | tf_op jit(solution)/shard_map/all_to_all | solution.py:23
  93.5 2.7 convolution_bitcast_fusion.2
  96.2 2.4 copy.15
  99.6 42.5 %all_to_all.16 = bf16[16,96,512]{2,1,0:T(8,128)(2,1)S(1)} all-to-all(bf16[16,96,512]{2,1,0:T(8,128)(2,1)S(1)} %stack.25), channel_id=1, replica_groups=mesh['row'=16,'col'=16] {'row'}, dimensions={0} | all-to-all | bytes 3145728 | tf_op jit(solution)/shard_map/all_to_all | solution.py:23
  142.1 4.6 convolution_bitcast_fusion
  146.7 2.4 copy.19
  149.3 42.7 %all_to_all.17 = bf16[16,96,512]{2,1,0:T(8,128)(2,1)S(1)} all-to-all(bf16[16,96,512]{2,1,0:T(8,128)(2,1)S(1)} %stack.23), channel_id=1, replica_groups=mesh['row'=16,'col'=16] {'row'}, dimensions={0} | all-to-all | bytes 3145728 | tf_op jit(solution)/shard_map/all_to_all | solution.py:23
  192.0 4.6 convolution_bitcast_fusion.1
  196.6 2.4 copy.17
  199.0 16.1 %reduce-scatter.13.cloned.1.call-done = f32[96,512]{1,0:T(8,128)} async-done(((f32[1536,512]{1,0:T(8,128)}), f32[96,512]{1,0:T(8,128)}) %reduce-scatter.13.cloned.1.call-update) | async-done | bytes 196624 | tf_op jit(solution)/shard_map/reduce_scatter | solution.py:26
  215.1 0.9 negate_bitcast_fusion.2
  216.1 89.7 %reduce-scatter.17.cloned.1.call-done = f32[96,512]{1,0:T(8,128)} async-done(((f32[1536,512]{1,0:T(8,128)}), f32[96,512]{1,0:T(8,128)}) %reduce-scatter.17.cloned.1.call-update) | async-done | bytes 196624 | tf_op jit(solution)/shard_map/reduce_scatter | solution.py:26
  305.8 0.9 negate_bitcast_fusion
  306.8 89.1 %reduce-scatter.15.cloned.1.call-done = f32[96,512]{1,0:T(8,128)} async-done(((f32[1536,512]{1,0:T(8,128)}), f32[96,512]{1,0:T(8,128)}) %reduce-scatter.15.cloned.1.call-update) | async-done | bytes 196624 | tf_op jit(solution)/shard_map/reduce_scatter | solution.py:26
  395.9 0.9 negate_bitcast_fusion.1
  397.5 3.1 fusion
  400.7 87.6 %reduce-scatter.11.cloned.1.call-done = f32[96,512]{1,0:T(8,128)} async-done(((f32[1536,512]{1,0:T(8,128)}), f32[96,512]{1,0:T(8,128)}) %reduce-scatter.11.cloned.1.call-update) | async-done | bytes 196624 | tf_op jit(solution)/shard_map/reduce_scatter | solution.py:33
  488.3 163.6 %all-reduce.2.cloned.1.call-done = f32[96,512]{1,0:T(8,128)} async-done(((f32[96,512]{1,0:T(8,128)}), f32[96,512]{1,0:T(8,128)}) %all-reduce.2.cloned.1.call-update) | async-done | bytes 196624 | tf_op jit(solution)/shard_map/psum | solution.py:34
  651.9 1.8 fusion.1
  653.7 89.9 %all-gather.2.cloned.1.call-done = f32[1536,512]{1,0:T(8,128)} async-done(((f32[96,512]{1,0:T(8,128)}), f32[1536,512]{1,0:T(8,128)}) %all-gather.2.cloned.1.call-update) | async-done | bytes 3145744 | tf_op jit(solution)/shard_map/all_gather | solution.py:35
  743.6 4.3 sub.13
  (31 shorter events, 4.5 us)
Async XLA Ops:
  7.2 208.0 %reduce-scatter.13.cloned.1.call-start = ((), (), s32[]{:S(2)}) async-start(), calls=%async_computation.10 | async-start | bytes 3342336 | tf_op jit(solution)/shard_map/reduce_scatter | solution.py:26
  8.9 84.7 %copy-start.3 = (bf16[1536,1536]{1,0:T(8,128)(2,1)S(1)}, bf16[1536,1536]{1,0:T(8,128)(2,1)}, u32[]{:S(2)}) copy-start(bf16[1536,1536]{1,0:T(8,128)(2,1)} %param.4) | copy-start | bytes 14155780
  10.1 36.0 %collective-permute-start = (bf16[3,96,512]{2,1,0:T(8,128)(2,1)S(1)}, bf16[3,96,512]{2,1,0:T(8,128)(2,1)S(1)}, u32[]{:S(2)}, u32[]{:S(2)}) collective-permute-start(bf16[3,96,512]{2,1,0:T(8,128)(2,1)S(1)} %bitcast_multiply_fusion), channel_id=1, source_target_pairs={{0,0},{1,16},{2,32},{3,48},{4,64},{5,80},{6,96},{7,112},{8,128},{9... | collective-permute-start | bytes 884744 | tf_op jit(solution)/shard_map/ppermute | solution.py:19
  98.6 0.9 copy-start.2
  98.6 207.2 %reduce-scatter.17.cloned.1.call-start = ((), (), s32[]{:S(2)}) async-start(), calls=%async_computation.12 | async-start | bytes 3342336 | tf_op jit(solution)/shard_map/reduce_scatter | solution.py:26
  149.1 246.8 %reduce-scatter.15.cloned.1.call-start = ((), (), s32[]{:S(2)}) async-start(), calls=%async_computation.11 | async-start | bytes 3342336 | tf_op jit(solution)/shard_map/reduce_scatter | solution.py:26
  199.0 289.3 %reduce-scatter.11.cloned.1.call-start = ((), (), s32[]{:S(2)}) async-start(), calls=%async_computation.7 | async-start | bytes 3342336 | tf_op jit(solution)/shard_map/reduce_scatter | solution.py:33
  396.8 0.7 copy-start.1
  400.6 343.0 %copy-start = (f32[3,512,512]{2,1,0:T(8,128)S(1)}, f32[3,512,512]{2,1,0:T(8,128)}, u32[]{:S(2)}) copy-start(f32[3,512,512]{2,1,0:T(8,128)} %param.6) | copy-start | bytes 9437188
  400.6 251.3 %all-reduce.2.cloned.1.call-start = ((), (), s32[]{:S(2)}) async-start(), calls=%async_computation.8 | async-start | bytes 393216 | tf_op jit(solution)/shard_map/psum | solution.py:34
  488.3 255.3 %all-gather.2.cloned.1.call-start = ((), (), s32[]{:S(2)}) async-start(), calls=%async_computation.9 | async-start | bytes 3342336 | tf_op jit(solution)/shard_map/all_gather | solution.py:35
Sparse Core Ops, SparseCore 0:
  98.7 116.3 reduce-scatter.12
  218.3 87.5 reduce-scatter.16
  308.4 87.4 reduce-scatter.14
  400.8 87.4 reduce-scatter.10
  490.7 161.1 all-reduce.1
  653.7 89.8 all-gather.1
